TPU v7x, 256 devices: a whole 4x4x8 slice. The times are simulated.
256 devices in a mesh: face: 32 (over z, y_lo, core), depth: 8 (over y_hi, x).
Axes of the slice: x: 4, y: 4 (y_hi: 2, y_lo: 2; y = y_hi * 2 + y_lo), z: 8, core: 2. Of those that a mesh axis runs over, the one named last changes fastest.
Arguments:
- thermal_field: float32 [2, 32, 8, 2048], P(None, 'face', 'depth'), may hold values from -6 to 6
- lumped_storage: float32 [2, 32, 8, 2048], P(None, 'face', 'depth'), may hold values from 1 to 4
- simplex_vertices: int32 [2, 32, 8, 4, 8192], P(None, 'face', 'depth'), may hold values from 0 to 2047
- stiffness_entries: float32 [2, 32, 8, 10, 8192], P(None, 'face', 'depth'), may hold values from -0.3 to 2, as said below
- interface_vertices: int32 [2, 32, 8, 2, 256], P(None, 'face', 'depth'), may hold values from 0 to 2047, as said below
- touching_triangle_vertices: int32 [2, 32, 3, 1024], P(None, 'face'), may hold values from 0 to 2047
- partner_lookup: int32 [32, 1024], replicated, may hold values from 0 to 32767, as said below
- engaged_flags: int32 [32, 1024], P('face'), may hold values 0 or 1
- rotor_gap_quantities: float32 [3, 32, 1024], P(None, 'face'), may hold values from -6 to 6
- lining_orthogonal_motion: float32 [32, 1024], P('face'), may hold values from -6 to 6
- touching_transfer_factor: float32 [32, 1024], P('face'), may hold values from 2 to 16
Outputs:
- advanced_thermal_field: float32 [2, 32, 8, 2048], P(None, 'face', 'depth')
- pressure: float32 [32, 1024], P('face')
Inputs may be any that keep to these rules, and one draw needn't show every extreme that they name: `stiffness_entries`: diagonal entries (the first four components) lie in [1, 2], off-diagonal ones in [-0.3, -0.05]. `interface_vertices`: the two lists of one body on one device name 512 different nodes. Position i of a block's upper list and position i of the lower list of the block above are copies of one node. `partner_lookup`: A disc face may meet a pad face of any patch; several disc faces may meet one pad face.
All inputs are finite; a program needn't handle non-finite values. No bound on the sum of `engaged_flags` on one device may be relied on, other than what follows from the above.
Results may differ from a plain program's by a relative error of at most 0.00002.
Values sent between devices are 32-bit elements; how exact they have to be, the bound alone decides.
No kernel may reach another device: no remote copies, remote signals or barrier semaphores. Data moves between devices by JAX's collectives and lax.ppermute only.
A program may use at most 64 MiB of HBM per device.

v0:
```python
import jax
import jax.numpy as jnp
from jax import lax
from jax.sharding import PartitionSpec as P

increment_factor = 0.05
nitsche = 1.0
film_floor = 0.25


def padded_2(cells, sides, width):
    for axis, dim in sides:
        count = lax.axis_size(axis)
        ends = count - 1
        head = lax.slice_in_dim(cells, 0, width, axis=dim)
        tail = lax.slice_in_dim(cells, cells.shape[dim] - width, cells.shape[dim], axis=dim)
        cells = jnp.concatenate(
            [
                lax.ppermute(tail, axis, [(i, (i + 1) % count) for i in range(ends)]),
                cells,
                lax.ppermute(head, axis, [((i + 1) % count, i) for i in range(ends)]),
            ],
            axis=dim,
        )
    return cells


def element_residual(values, corners, entries):
    picked = values[corners]
    row_one = (
        entries[0] * picked[0]
        + entries[4] * picked[1]
        + entries[5] * picked[2]
        + entries[6] * picked[3]
    )
    row_two = (
        entries[4] * picked[0]
        + entries[1] * picked[1]
        + entries[7] * picked[2]
        + entries[8] * picked[3]
    )
    row_three = (
        entries[5] * picked[0]
        + entries[7] * picked[1]
        + entries[2] * picked[2]
        + entries[9] * picked[3]
    )
    row_four = (
        entries[6] * picked[0]
        + entries[8] * picked[1]
        + entries[9] * picked[2]
        + entries[3] * picked[3]
    )
    stacked = -jnp.stack([row_one, row_two, row_three, row_four])
    return jax.ops.segment_sum(
        stacked.reshape(-1), corners.reshape(-1), num_segments=values.shape[0]
    )


def touching_triangle_values(values, corners):
    picked = values[corners]
    return (picked[0] + picked[1] + picked[2]) / 3.0


def spread_faces(face_rates, corners, solid_vertex_total):
    shares = jnp.broadcast_to(face_rates / 3.0, corners.shape)
    return jax.ops.segment_sum(
        shares.reshape(-1), corners.reshape(-1), num_segments=solid_vertex_total
    )


def set_rims(values, low_at, up_at, low_set, up_set):
    return values.at[low_at].set(low_set).at[up_at].set(up_set)


def local(
    thermal_field,
    lumped_storage,
    simplex_vertices,
    stiffness_entries,
    interface_vertices,
    touching_triangle_vertices,
    partner_lookup,
    engaged_flags,
    rotor_gap_quantities,
    lining_orthogonal_motion,
    touching_transfer_factor,
):
    solid_vertex_total = thermal_field.shape[-1]
    patch_index = lax.axis_index("face")
    depth_index = lax.axis_index("depth")
    surface = (depth_index == 0).astype(jnp.float32)
    thermal_imbalance = jnp.stack(
        [
            element_residual(
                thermal_field[solid_selector, 0, 0],
                simplex_vertices[solid_selector, 0, 0],
                stiffness_entries[solid_selector, 0, 0],
            )
            for solid_selector in range(2)
        ]
    )
    rotor_triangle_values = touching_triangle_values(
        thermal_field[0, 0, 0], touching_triangle_vertices[0, 0]
    )
    lining_triangle_values = touching_triangle_values(
        thermal_field[1, 0, 0], touching_triangle_vertices[1, 0]
    )
    active_mask = engaged_flags[0].astype(jnp.float32)
    displace = rotor_gap_quantities[0, 0]
    opening = rotor_gap_quantities[1, 0]
    multiplier = rotor_gap_quantities[2, 0]
    weight = active_mask * touching_transfer_factor[0]
    own_match = lax.dynamic_slice_in_dim(partner_lookup, patch_index, 1, 0)[0]
    pad_normals, pad_traces = (
        lax.all_gather(lining_orthogonal_motion[0], "face", axis=0, tiled=True),
        lax.all_gather(lining_triangle_values, "face", axis=0, tiled=True),
    )
    pressure = active_mask * jnp.maximum(
        multiplier + nitsche * (displace - pad_normals[own_match] - opening), 0.0
    )
    disc_rate = weight * (film_floor + pressure) * (pad_traces[own_match] - rotor_triangle_values)
    spread = jax.ops.segment_sum(disc_rate, own_match, num_segments=partner_lookup.size)
    pad_rate = -lax.psum_scatter(spread, "face", scatter_dimension=0, tiled=True)
    nodal = jnp.stack(
        [
            spread_faces(disc_rate, touching_triangle_vertices[0, 0], solid_vertex_total),
            spread_faces(pad_rate, touching_triangle_vertices[1, 0], solid_vertex_total),
        ]
    )
    thermal_imbalance = thermal_imbalance + surface * nodal
    lower = interface_vertices[:, 0, 0, 0]
    upper = interface_vertices[:, 0, 0, 1]
    low_values = jnp.take_along_axis(thermal_imbalance, lower, axis=1)
    up_values = jnp.take_along_axis(thermal_imbalance, upper, axis=1)
    rows_both = jnp.stack([low_values.reshape(-1), up_values.reshape(-1)])
    padded = padded_2(rows_both, (("depth", 0),), 1)
    low_new = low_values + padded[0].reshape(low_values.shape)
    up_new = up_values + padded[3].reshape(up_values.shape)
    gathered_imbalance = jax.vmap(set_rims)(thermal_imbalance, lower, upper, low_new, up_new)
    advanced_thermal_field = (
        thermal_field + increment_factor * gathered_imbalance[:, None, None, :] / lumped_storage
    )
    return (advanced_thermal_field, pressure[None])


def solution(mesh):
    placed = (
        P(None, "face", "depth", None),
        P(None, "face", "depth", None),
        P(None, "face", "depth", None, None),
        P(None, "face", "depth", None, None),
        P(None, "face", "depth", None, None),
        P(None, "face", None, None),
        P(),
        P("face", None),
        P(None, "face", None),
        P("face", None),
        P("face", None),
    )
    return jax.shard_map(
        local,
        mesh=mesh,
        in_specs=placed,
        out_specs=(P(None, "face", "depth", None), P("face", None)),
        check_vma=False,
    )
```

profile of v0, /device:TPU:24, one launch (start us, length us, event | category | flops | bytes accessed | tf_op | source)
XLA Modules:
  0.0 958.9 jit_solution(17797581546140559378)
XLA Ops:
  7.2 0.7 fusion.56
  7.9 0.8 compare_select_fusion.4
  8.8 17.4 %gather_fusion.3 = f32[3072]{0:T(1024)S(1)} fusion(f32[2048]{0:T(1024)S(1)} %bitcast.281, s32[3072]{0:T(1024)S(1)} %broadcast_clamp_fusion.3), kind=kCustom, calls=%fused_computation.5 | custom fusion | bytes 36864 | tf_op jit(solution)/shard_map/gather | solution.py:61
  26.2 34.7 %all-gather.1 = f32[1,32768]{1,0:T(1,128)S(1)} all-gather(f32[1,1024]{1,0:T(1,128)S(1)} %bitcast.324), channel_id=3, replica_groups=mesh['face'=32,'depth'=8] {'face'}, dimensions={1}, use_global_device_ids=true | all-gather | bytes 135168 | tf_op jit(solution)/shard_map/all_gather | solution.py:117
  60.9 34.0 %all-gather = f32[1,32768]{1,0:T(1,128)S(1)} all-gather(f32[1,1024]{1,0:T(1,128)S(1)} %copy-done.8), channel_id=2, replica_groups=mesh['face'=32,'depth'=8] {'face'}, dimensions={1}, use_global_device_ids=true | all-gather | bytes 135168 | tf_op jit(solution)/shard_map/all_gather | solution.py:116
  94.9 6.1 gather_fusion.4
  101.1 6.2 gather_fusion.2
  107.3 0.7 copy-done.4
  108.6 17.4 %gather_fusion.5 = f32[3072]{0:T(1024)S(1)} fusion(f32[2048]{0:T(1024)S(1)} %bitcast.279, s32[3072]{0:T(1024)S(1)} %broadcast_clamp_fusion.2), kind=kCustom, calls=%fused_computation.7 | custom fusion | bytes 36864 | tf_op jit(solution)/shard_map/gather | solution.py:61
  126.1 6.5 scatter_custom_fusion.3
  132.8 180.5 %gather_fusion.1 = f32[32768]{0:T(1024)S(1)} fusion(f32[2048]{0:T(1024)S(1)} %bitcast.282, s32[32768]{0:T(1024)S(1)} %broadcast_clamp_fusion), kind=kCustom, calls=%fused_computation.3 | custom fusion | bytes 393216 | tf_op jit(solution)/shard_map/gather | solution.py:29
  313.4 180.5 %gather_fusion = f32[32768]{0:T(1024)S(1)} fusion(f32[2048]{0:T(1024)S(1)} %bitcast.280, s32[32768]{0:T(1024)S(1)} %broadcast_clamp_fusion.1), kind=kCustom, calls=%fused_computation.2 | custom fusion | bytes 393216 | tf_op jit(solution)/shard_map/gather | solution.py:29
  495.7 172.3 %scatter_custom_fusion = f32[2048]{0:T(1024)S(1)} fusion(s32[32768]{0:T(1024)S(1)} %bitcast.308, f32[32768]{0:T(1024)S(1)} %bitcast.307, f32[]{:T(128)} %constant.19.clone.1), kind=kCustom, calls=%fused_computation.121 | custom fusion | flops 32768 | bytes 8196 | tf_op jit(solution)/shard_map/scatter-add | solution.py:55
  668.1 172.3 %scatter_custom_fusion.1 = f32[2048]{0:T(1024)S(1)} fusion(s32[32768]{0:T(1024)S(1)} %bitcast.310, f32[32768]{0:T(1024)S(1)} %bitcast.309, f32[]{:T(128)} %constant.19.clone.1), kind=kCustom, calls=%fused_computation.119 | custom fusion | flops 32768 | bytes 8196 | tf_op jit(solution)/shard_map/scatter-add | solution.py:55
  842.3 16.7 %scatter_custom_fusion.2 = f32[2048]{0:T(1024)S(1)} fusion(s32[3072]{0:T(1024)S(1)} %bitcast.326, f32[3072]{0:T(1024)S(1)} %reshape.422, f32[]{:T(128)} %constant.19.clone.1), kind=kCustom, calls=%fused_computation.117 | custom fusion | flops 3072 | bytes 8196 | tf_op jit(solution)/shard_map/scatter-add | solution.py:67
  859.0 0.7 fusion.38
  859.7 16.7 %scatter_custom_fusion.4 = f32[2048]{0:T(1024)S(1)} fusion(s32[3072]{0:T(1024)S(1)} %bitcast.325, f32[3072]{0:T(1024)S(1)} %reshape.438, f32[]{:T(128)} %constant.19.clone.1), kind=kCustom, calls=%fused_computation.115 | custom fusion | flops 3072 | bytes 8196 | tf_op jit(solution)/shard_map/scatter-add | solution.py:67
  876.5 4.8 gather_fusion.6
  881.4 5.6 collective-permute-start.1
  887.5 4.8 gather_fusion.7
  893.6 1.9 collective-permute-start
  895.6 7.1 collective-permute-done
  903.4 24.0 %scatter_fusion = f32[2,2048]{1,0:T(2,128)S(1)} fusion(f32[2,2048]{1,0:T(2,128)S(1)} %maximum_add_fusion, s32[512]{0:T(512)S(1)} %bitcast.286, f32[512]{0:T(512)S(1)} %bitcast.328), kind=kCustom, calls=%fused_computation.13 | custom fusion | bytes 10240 | tf_op jit(solution)/shard_map/vmap()/scatter | solution.py:73
  927.4 24.0 %scatter_fusion.1 = f32[2,2048]{1,0:T(2,128)S(1)} fusion(f32[2,2048]{1,0:T(2,128)S(1)} %scatter_fusion, s32[512]{0:T(512)S(1)} %bitcast.285, f32[512]{0:T(512)S(1)} %bitcast.327), kind=kCustom, calls=%fused_computation.14 | custom fusion | bytes 10240 | tf_op jit(solution)/shard_map/vmap()/scatter | solution.py:73
  (78 shorter events, 7.2 us)
Async XLA Ops:
  7.2 851.9 %all-reduce.3.cloned.1.call-start = ((), (), s32[]{:S(2)}) async-start(), calls=%async_computation | async-start | bytes 262144
  7.9 0.8 copy-start.2
  26.2 34.7 %copy-start.8 = (f32[1,1024]{1,0:T(1,128)S(1)}, f32[1,1024]{1,0:T(1,128)}, u32[]{:S(2)}) copy-start(f32[1,1024]{1,0:T(1,128)} %param.22) | copy-start | bytes 12292
  107.2 0.7 copy-start.4
  107.9 0.7 copy-start.6
  108.6 17.4 %copy-start.9 = (f32[1,1024]{1,0:T(1,128)S(1)}, f32[1,1024]{1,0:T(1,128)}, u32[]{:S(2)}) copy-start(f32[1,1024]{1,0:T(1,128)} %param.23) | copy-start | bytes 12292
  126.1 6.6 copy-start.1
  313.4 180.6 %copy-start = (f32[2,1,1,10,8192]{4,2,3,1,0:T(1,128)S(1)}, f32[2,1,1,10,8192]{4,2,3,1,0:T(1,128)}, u32[]{:S(2)}) copy-start(f32[2,1,1,10,8192]{4,2,3,1,0:T(1,128)} %param.16) | copy-start | bytes 1966084
  495.0 0.7 copy-start.5
  840.4 0.7 copy-start.10
  881.4 11.0 %collective-permute-start.1 = (f32[1,512]{1,0:T(1,128)S(1)}, f32[1,512]{1,0:T(1,128)S(1)}, u32[]{:S(2)}, u32[]{:S(2)}) collective-permute-start(f32[1,512]{1,0:T(1,128)S(1)} %bitcast.332), channel_id=1, source_target_pairs={{1,0},{2,1},{3,2},{4,3},{5,4},{6,5},{7,6},{9,8},{10,9},{11,10},{12... | collective-permute-start | bytes 6152 | tf_op jit(solution)/shard_map/ppermute | solution.py:21
  893.6 9.1 collective-permute-start
  927.4 24.0 %copy-start.3 = (f32[2,1,1,2048]{3,2,1,0:T(1,128)S(1)}, f32[2,1,1,2048]{3,2,1,0:T(1,128)}, u32[]{:S(2)}) copy-start(f32[2,1,1,2048]{3,2,1,0:T(1,128)} %param.13) | copy-start | bytes 49156
  927.4 24.0 %copy-start.7 = (f32[2,1,1,2048]{3,2,1,0:T(1,128)S(1)}, f32[2,1,1,2048]{3,2,1,0:T(1,128)}, u32[]{:S(2)}) copy-start(f32[2,1,1,2048]{3,2,1,0:T(1,128)} %param.14) | copy-start | bytes 49156
Sparse Core Ops, SparseCore 0:
  132.8 197.5 all-reduce.2
where the time goes:
time: 959 us
  local copies, waits for them, and re-layouts  471 us (49%)
  other arithmetic  389 us (41%)
  blocking collectives  68.7 us (7%)
  between operations  15.2 us (2%)
    gather x2, local copies, waits for them, and re-layouts, element_residual(): picked = values[corners]  361 us
    scatter-add x2, other arithmetic, element_residual(): jax.ops.segment_sum(stacked.reshape(-1), corners.reshape(-1), num_segment...  345 us
    scatter x2, local copies, waits for them, and re-layouts, set_rims(): return values.at[low_at].set(low_set).at[up_at].set(up_set)  47.9 us
    gather x2, local copies, waits for them, and re-layouts, touching_triangle_values(): picked = values[corners]  34.8 us
    all_gather x1, blocking collectives, local(): lax.all_gather(lining_triangle_values, 'face', axis=0, tiled=True)  34.7 us
    all_gather x1, blocking collectives, local(): lax.all_gather(lining_orthogonal_motion[0], 'face', axis=0, tiled=True)  34 us
    scatter-add x2, other arithmetic, spread_faces(): jax.ops.segment_sum(shares.reshape(-1), corners.reshape(-1), num_segments...  33.4 us
  transfers between devices with their start and end apart: 3, of which 1 were waited for; matrix products, arithmetic and copies ran while one was open for 76% of the time, Pallas kernels for 0%

commit v1 on v0

--- a/solution.py
+++ b/solution.py
@@ -112,9 +112,18 @@
     multiplier = rotor_gap_quantities[2, 0]
     weight = active_mask * touching_transfer_factor[0]
     own_match = lax.dynamic_slice_in_dim(partner_lookup, patch_index, 1, 0)[0]
+    tell_roads = lambda array_here, group_axis, on_dim: jnp.concatenate(
+        lax.all_to_all(
+            jnp.stack([array_here for _ in range(lax.psum(1, axis_name=group_axis))], axis=0),
+            axis_name=group_axis,
+            split_axis=0,
+            concat_axis=0,
+        ),
+        axis=on_dim,
+    )
     pad_normals, pad_traces = (
         lax.all_gather(lining_orthogonal_motion[0], "face", axis=0, tiled=True),
-        lax.all_gather(lining_triangle_values, "face", axis=0, tiled=True),
+        tell_roads(lining_triangle_values, "face", 0),
     )
     pressure = active_mask * jnp.maximum(
         multiplier + nitsche * (displace - pad_normals[own_match] - opening), 0.0

time: 959 us -> 1120 us (1.17)
  waiting for transfers between devices: 7.17 us -> 193 us
  blocking collectives: 68.7 us -> 31.3 us
    unnamed x2, waiting for transfers between devices: 0.04 us -> 185 us
    all_gather x1 -> x0, blocking collectives: 34.7 us -> none  [local(): lax.all_gather(lining_triangle_values, 'face', axis=0, tiled=True)]
  transfers between devices with their start and end apart: 3 -> 4, of which waited for: 1 -> 2; matrix products, arithmetic and copies ran while one was open for 76% -> 67% of each run, Pallas kernels for 0% -> 0%
where the time goes in v1:
time: 1120 us
  local copies, waits for them, and re-layouts  472 us (42%)
  other arithmetic  389 us (35%)
  waiting for transfers between devices  193 us (17%)
  blocking collectives  31.3 us (3%)
  starting transfers between devices  17.2 us (2%)
  between operations  15.2 us (1%)
    gather x2, local copies, waits for them, and re-layouts, element_residual(): picked = values[corners]  361 us
    scatter-add x2, other arithmetic, element_residual(): jax.ops.segment_sum(stacked.reshape(-1), corners.reshape(-1), num_segment...  345 us
    unnamed x2, waiting for transfers between devices  185 us
    scatter x2, local copies, waits for them, and re-layouts, set_rims(): return values.at[low_at].set(low_set).at[up_at].set(up_set)  47.9 us
    gather x2, local copies, waits for them, and re-layouts, touching_triangle_values(): picked = values[corners]  34.8 us
    scatter-add x2, other arithmetic, spread_faces(): jax.ops.segment_sum(shares.reshape(-1), corners.reshape(-1), num_segments...  33.4 us
    all_gather x1, blocking collectives, local(): lax.all_gather(lining_orthogonal_motion[0], 'face', axis=0, tiled=True)  31.3 us
  transfers between devices with their start and end apart: 4, of which 2 were waited for; matrix products, arithmetic and copies ran while one was open for 67% of the time, Pallas kernels for 0%

profile of v1, /device:TPU:24, one launch (start us, length us, event | category | flops | bytes accessed | tf_op | source)
XLA Modules:
  0.0 1117.2 jit_solution(14202721247319395673)
XLA Ops:
  7.2 0.7 fusion.56
  7.9 17.4 %gather_fusion.3 = f32[3072]{0:T(1024)S(1)} fusion(f32[2048]{0:T(1024)S(1)} %bitcast.280, s32[3072]{0:T(1024)S(1)} %broadcast_clamp_fusion.3), kind=kCustom, calls=%fused_computation.5 | custom fusion | bytes 36864 | tf_op jit(solution)/shard_map/gather | solution.py:61
  25.4 0.7 stack.23
  26.1 10.1 all-to-all-start
  36.4 180.5 %gather_fusion.1 = f32[32768]{0:T(1024)S(1)} fusion(f32[2048]{0:T(1024)S(1)} %bitcast.281, s32[32768]{0:T(1024)S(1)} %broadcast_clamp_fusion), kind=kCustom, calls=%fused_computation.3 | custom fusion | bytes 393216 | tf_op jit(solution)/shard_map/gather | solution.py:29
  217.0 180.5 %gather_fusion = f32[32768]{0:T(1024)S(1)} fusion(f32[2048]{0:T(1024)S(1)} %bitcast.278, s32[32768]{0:T(1024)S(1)} %broadcast_clamp_fusion.1), kind=kCustom, calls=%fused_computation.2 | custom fusion | bytes 393216 | tf_op jit(solution)/shard_map/gather | solution.py:29
  398.2 0.8 compare_select_fusion.4
  400.4 31.3 %all-gather = f32[1,32768]{1,0:T(1,128)S(1)} all-gather(f32[1,1024]{1,0:T(1,128)S(1)} %copy-done.8), channel_id=2, replica_groups=mesh['face'=32,'depth'=8] {'face'}, dimensions={1}, use_global_device_ids=true | all-gather | bytes 135168 | tf_op jit(solution)/shard_map/all_gather | solution.py:125
  431.8 17.4 %gather_fusion.5 = f32[3072]{0:T(1024)S(1)} fusion(f32[2048]{0:T(1024)S(1)} %bitcast.279, s32[3072]{0:T(1024)S(1)} %broadcast_clamp_fusion.2), kind=kCustom, calls=%fused_computation.7 | custom fusion | bytes 36864 | tf_op jit(solution)/shard_map/gather | solution.py:61
  449.3 172.3 %scatter_custom_fusion = f32[2048]{0:T(1024)S(1)} fusion(s32[32768]{0:T(1024)S(1)} %bitcast.307, f32[32768]{0:T(1024)S(1)} %bitcast.306, f32[]{:T(128)} %constant.19.clone.1), kind=kCustom, calls=%fused_computation.121 | custom fusion | flops 32768 | bytes 8196 | tf_op jit(solution)/shard_map/scatter-add | solution.py:55
  621.6 172.3 %scatter_custom_fusion.1 = f32[2048]{0:T(1024)S(1)} fusion(s32[32768]{0:T(1024)S(1)} %bitcast.309, f32[32768]{0:T(1024)S(1)} %bitcast.308, f32[]{:T(128)} %constant.19.clone.1), kind=kCustom, calls=%fused_computation.119 | custom fusion | flops 32768 | bytes 8196 | tf_op jit(solution)/shard_map/scatter-add | solution.py:55
  793.9 6.2 gather_fusion.2
  802.0 6.2 gather_fusion.4
  808.9 6.5 scatter_custom_fusion.3
  815.5 16.7 %scatter_custom_fusion.2 = f32[2048]{0:T(1024)S(1)} fusion(s32[3072]{0:T(1024)S(1)} %bitcast.324, f32[3072]{0:T(1024)S(1)} %reshape.430, f32[]{:T(128)} %constant.19.clone.1), kind=kCustom, calls=%fused_computation.117 | custom fusion | flops 3072 | bytes 8196 | tf_op jit(solution)/shard_map/scatter-add | solution.py:67
  832.2 185.5 %all-reduce.3.cloned.1.call-done = f32[32768]{0:T(1024)} async-done(((f32[32768]{0:T(1024)}), f32[32768]{0:T(1024)}) %all-reduce.3.cloned.1.call-update) | async-done | bytes 131088
  1018.4 16.7 %scatter_custom_fusion.4 = f32[2048]{0:T(1024)S(1)} fusion(s32[3072]{0:T(1024)S(1)} %bitcast.323, f32[3072]{0:T(1024)S(1)} %reshape.446, f32[]{:T(128)} %constant.19.clone.1), kind=kCustom, calls=%fused_computation.115 | custom fusion | flops 3072 | bytes 8196 | tf_op jit(solution)/shard_map/scatter-add | solution.py:67
  1035.1 4.8 gather_fusion.6
  1040.0 5.2 collective-permute-start.1
  1045.8 4.8 gather_fusion.7
  1051.9 1.9 collective-permute-start
  1053.8 7.1 collective-permute-done
  1061.7 24.0 %scatter_fusion = f32[2,2048]{1,0:T(2,128)S(1)} fusion(f32[2,2048]{1,0:T(2,128)S(1)} %maximum_add_fusion, s32[512]{0:T(512)S(1)} %bitcast.285, f32[512]{0:T(512)S(1)} %bitcast.326), kind=kCustom, calls=%fused_computation.13 | custom fusion | bytes 10240 | tf_op jit(solution)/shard_map/vmap()/scatter | solution.py:73
  1085.6 24.0 %scatter_fusion.1 = f32[2,2048]{1,0:T(2,128)S(1)} fusion(f32[2,2048]{1,0:T(2,128)S(1)} %scatter_fusion, s32[512]{0:T(512)S(1)} %bitcast.284, f32[512]{0:T(512)S(1)} %bitcast.325), kind=kCustom, calls=%fused_computation.14 | custom fusion | bytes 10240 | tf_op jit(solution)/shard_map/vmap()/scatter | solution.py:73
  (80 shorter events, 8.3 us)
Async XLA Ops:
  7.2 0.7 copy-start.2
  25.4 10.9 copy-start.1
  26.1 775.9 %all-to-all-start = ((f32[32,1,1024]{2,1,0:T(1,128)}), f32[32,1,1024]{2,1,0:T(1,128)S(1)}, u32[]{:S(2)}, u32[]{:S(2)}) async-start(f32[32,1,1024]{2,1,0:T(1,128)} %stack.23), calls=%async_computation | async-start | bytes 262144 | tf_op jit(solution)/shard_map/all_to_all | solution.py:116
  36.2 981.5 %all-reduce.3.cloned.1.call-start = ((), (), s32[]{:S(2)}) async-start(), calls=%async_computation.1 | async-start | bytes 262144
  217.0 180.6 %copy-start = (f32[2,1,1,10,8192]{4,2,3,1,0:T(1,128)S(1)}, f32[2,1,1,10,8192]{4,2,3,1,0:T(1,128)}, u32[]{:S(2)}) copy-start(f32[2,1,1,10,8192]{4,2,3,1,0:T(1,128)} %param.16) | copy-start | bytes 1966084
  399.0 0.7 copy-start.5
  399.7 0.7 copy-start.8
  431.8 17.4 %copy-start.6 = (s32[1,1024]{1,0:T(1,128)S(1)}, s32[1,1024]{1,0:T(1,128)}, u32[]{:S(2)}) copy-start(s32[1,1024]{1,0:T(1,128)} %param.20) | copy-start | bytes 12292
  800.1 1.9 copy-start.4
  800.1 0.7 copy-start.10
  808.2 0.7 copy-start.9
  1040.0 10.6 collective-permute-start.1
  1051.9 9.1 collective-permute-start
  1085.6 24.0 %copy-start.3 = (f32[2,1,1,2048]{3,2,1,0:T(1,128)S(1)}, f32[2,1,1,2048]{3,2,1,0:T(1,128)}, u32[]{:S(2)}) copy-start(f32[2,1,1,2048]{3,2,1,0:T(1,128)} %param.13) | copy-start | bytes 49156
  1085.6 24.0 %copy-start.7 = (f32[2,1,1,2048]{3,2,1,0:T(1,128)S(1)}, f32[2,1,1,2048]{3,2,1,0:T(1,128)}, u32[]{:S(2)}) copy-start(f32[2,1,1,2048]{3,2,1,0:T(1,128)} %param.14) | copy-start | bytes 49156
Sparse Core Ops, SparseCore 0:
  815.6 202.0 all-reduce.2
